TPU v7x, 32 devices: a whole 2x2x4 slice. The times are simulated.
32 devices in a mesh: vol: 1, slab: 8 (over z, x), filt: 4 (over y, core).
Axes of the slice: x: 2, y: 2, z: 4, core: 2. Of those that a mesh axis runs over, the one named last changes fastest.
Arguments:
- volume: bfloat16 [32, 64, 64, 256], P(('vol', 'slab', 'filt')), may hold values from -6 to 6
- weights: bfloat16 [256, 27, 256], P('filt'), may hold values from -0.078125 to 0.078125
- bias: bfloat16 [256], P('filt'), may hold values from -3 to 3
Outputs:
- activated: bfloat16 [32, 64, 64, 256], P(('vol', 'slab'), None, None, 'filt')
All inputs are finite; a program needn't handle non-finite values.
Results may differ from a plain program's by a relative error of at most 0.001.
Values may be sent and summed in bfloat16 or wider, within the bound.
A program may use at most 448 MiB of HBM per device.

v0:
```python
import jax
import jax.numpy as jnp
from jax import lax
from jax.sharding import PartitionSpec as P


def extended(cells, sides, width):
    for axis, dim in sides:
        count = lax.axis_size(axis)
        ends = count - 1
        head = lax.slice_in_dim(cells, 0, width, axis=dim)
        tail = lax.slice_in_dim(cells, cells.shape[dim] - width, cells.shape[dim], axis=dim)
        cells = jnp.concatenate(
            [
                lax.ppermute(tail, axis, [(i, (i + 1) % count) for i in range(ends)]),
                cells,
                lax.ppermute(head, axis, [((i + 1) % count, i) for i in range(ends)]),
            ],
            axis=dim,
        )
    return cells


def convolve(padded, weights, bias):
    planes = padded.shape[0] - 2
    rows = padded.shape[1]
    cols = padded.shape[2]
    chans = padded.shape[3]
    outs = weights.shape[0]
    framed = jnp.pad(padded, ((0, 0), (1, 1), (1, 1), (0, 0)))
    total = jnp.zeros((planes, rows * cols, outs), jnp.float32)
    for tap_z in range(3):
        for tap_y in range(3):
            for tap_x in range(3):
                window = framed[
                    tap_z : tap_z + planes, tap_y : tap_y + rows, tap_x : tap_x + cols
                ].reshape(planes, rows * cols, chans)
                tap_weight = weights[:, 9 * tap_z + 3 * tap_y + tap_x, :]
                total = total + jnp.einsum(
                    "zpi,oi->zpo", window, tap_weight, preferred_element_type=jnp.float32
                )
    shifted = total + bias.astype(jnp.float32)[None, None, :]
    result = jnp.where(shifted > 0, shifted, 0.3 * shifted)
    return result.astype(jnp.bfloat16).reshape(planes, rows, cols, outs)


def body(volume, weights, bias):
    slab_planes = lax.all_gather(volume, "filt", axis=0, tiled=True)
    padded = extended(slab_planes, (("slab", 0),), 1)
    return convolve(padded, weights, bias)


def solution(mesh):
    return jax.shard_map(
        body,
        mesh=mesh,
        in_specs=(P(("vol", "slab", "filt"), None, None, None), P("filt", None, None), P("filt")),
        out_specs=P(("vol", "slab"), None, None, "filt"),
        check_vma=False,
    )
```

profile of v0, /device:TPU:0, one launch (start us, length us, event | category | flops | bytes accessed | tf_op | source)
XLA Modules:
  0.0 524.3 jit_solution(2084521685995472989)
XLA Ops:
  7.3 62.7 %all-gather.2.cloned.1.call-done = bf16[4,64,64,256]{3,2,1,0:T(8,128)(2,1)} async-done(((bf16[1,64,64,256]{3,2,1,0:T(8,128)(2,1)}), bf16[4,64,64,256]{3,2,1,0:T(8,128)(2,1)}) %all-gather.2.cloned.1.call-update) | async-done | bytes 8388624 | tf_op jit(solution)/shard_map/all_gather | solution.py:48
  78.4 4.6 fusion.57
  82.9 83.6 %collective-permute-done = bf16[1,64,64,256]{3,2,1,0:T(8,128)(2,1)S(1)} collective-permute-done((bf16[1,64,64,256]{3,2,1,0:T(8,128)(2,1)S(1)}, bf16[1,64,64,256]{3,2,1,0:T(8,128)(2,1)S(1)}, u32[]{:S(2)}, u32[]{:S(2)}) %collective-permute-start) | collective-permute-done | bytes 2097184 | tf_op jit(solution)/shard_map/ppermute | solution.py:15
  169.3 21.5 %select_maximum_fusion = bf16[6,66,66,256]{3,2,1,0:T(8,128)(2,1)} fusion(bf16[1,64,64,256]{3,2,1,0:T(8,128)(2,1)S(1)} %collective-permute-done.1, bf16[4,64,64,256]{3,2,1,0:T(8,128)(2,1)S(1)} %copy-done, bf16[1,64,64,256]{3,2,1,0:T(8,128)(2,1)S(1)} %collective-permute-done), kind=kLoop, calls=%fused_computation.7 | loop fusion | flops 127125504 | bytes 25964544 | tf_op jit(solution)/shard_map/concatenate | solution.py:13
  190.8 126.1 %fusion.111 = (bf16[4,64,64,256]{3,2,1,0:T(8,128)(2,1)}, bf16[4,64,64,256]{3,2,1,0:T(8,128)(2,1)}, bf16[4,64,64,256]{3,2,1,0:T(8,128)(2,1)}, bf16[4,64,64,256]{3...) fusion(bf16[6,66,66,256]{3,2,1,0:T(8,128)(2,1)} %select_maximum, ...), kind=kLoop, calls=%fused_computation.122 | loop fusion | bytes 318767104 | tf_op jit(solution)/shard_map/slice | solution.py:35
  316.9 32.3 %fusion.112 = (bf16[4,64,64,256]{3,2,1,0:T(8,128)(2,1)}, bf16[4,64,64,256]{3,2,1,0:T(8,128)(2,1)}, bf16[4,64,64,256]{3,2,1,0:T(8,128)(2,1)}, bf16[4,64,64,256]{3,2,1,0:T(8,128)(2,1)}, bf16[4,64,64,256]{3,2,1,0:T(8,128)(2,1)}) fusion(bf16[6,66,66,256]{3,2,1,0:T(8,128)(2,1)} %select_maximum_fusion), kind=kLoop, calls=%fused_computation.123 | loop fusion | bytes 83886080 | tf_op jit(solution)/shard_map/slice | solution.py:35
  349.2 8.2 %fusion.59 = f32[4,4096,64]{1,2,0:T(8,128)} fusion(bf16[4,4096,256]{2,1,0:T(8,128)(2,1)} %bitcast.221, bf16[64,27,256]{2,0,1:T(8,128)(2,1)S(1)} %copy-done.6), kind=kOutput, calls=%fused_computation.70 | convolution fusion | flops 536870912 | bytes 12615680 | tf_op jit(solution)/shard_map/zpi,oi->zpo/dot_general | solution.py:39
  357.4 4.6 fusion.61
  362.1 4.7 fusion.63
  366.8 4.6 fusion.65
  371.5 4.7 fusion.67
  376.1 4.6 fusion.69
  380.7 4.7 fusion.71
  385.4 4.6 fusion.73
  390.0 4.7 fusion.77
  394.8 4.6 fusion.79
  399.4 4.8 fusion.81
  408.6 4.6 fusion.75
  413.2 4.6 fusion.34
  417.8 4.6 fusion.36
  422.4 4.6 fusion.38
  431.6 4.6 fusion.44
  436.2 4.6 fusion.46
  440.8 4.6 fusion.48
  445.4 4.7 fusion.50
  450.2 4.6 fusion.52
  454.8 4.6 fusion.54
  459.3 4.7 fusion.32
  464.0 4.6 fusion.40
  468.6 24.2 %fusion.29 = f32[4,4096,64]{1,2,0:T(8,128)} fusion(f32[4,4096,64]{1,2,0:T(8,128)} %fusion.57, f32[4,4096,64]{1,2,0:T(8,128)} %fusion.59, f32[4,4096,64]{1,2,0:T(8,128)} %fusion.61, f32[4,4096,64]{1,2,0:T(8,128)} %fusion.63, f32[4,4096,64]{1,2,0:T(8,128)} %fusion.65, f32[4,4096,64]{1,2,0:T(8,128)} %fusion.67, f32[4,4096,64]{1,2,0:T(8,128)} %fusion.69, ...), kind=kOutput, calls=%fused_computation.40 | convolution fusion | flops 550502400 | bytes 67141632 | tf_op jit(solution)/shard_map/zpi,oi->zpo/dot_general | solution.py:39
  492.8 19.7 %fusion.31 = bf16[4,4096,64]{1,2,0:T(8,128)(2,1)} fusion(f32[4,4096,64]{1,2,0:T(8,128)} %fusion.32, f32[4,4096,64]{1,2,0:T(8,128)} %fusion.34, f32[4,4096,64]{1,2,0:T(8,128)} %fusion.36, f32[4,4096,64]{1,2,0:T(8,128)} %fusion.38, f32[4,4096,64]{1,2,0:T(8,128)} %fusion.40, f32[4,4096,64]{1,2,0:T(8,128)} %fusion.42, f32[4,4096,64]{1,2,0:T(8,128)} %fusion.44, ...), kind=kOutput, calls=%fused_computation.42 | convolution fusion | flops 555745280 | bytes 65044992 | tf_op jit(solution)/shard_map/zpi,oi->zpo/dot_general | solution.py:39
  512.5 4.8 copy.6
  (142 shorter events, 21.0 us)
Async XLA Ops:
  6.5 71.2 %copy-start.8 = (bf16[64]{0:T(256)(128)(2,1)S(1)}, bf16[64]{0:T(256)(128)(2,1)}, u32[]{:S(2)}) copy-start(bf16[64]{0:T(256)(128)(2,1)} %param.5) | copy-start | bytes 388
  6.5 71.8 %copy-start.6 = (bf16[64,27,256]{2,0,1:T(8,128)(2,1)S(1)}, bf16[64,27,256]{2,0,1:T(8,128)(2,1)}, u32[]{:S(2)}) copy-start(bf16[64,27,256]{2,0,1:T(8,128)(2,1)} %param.4) | copy-start | bytes 2654212
  6.5 63.4 %all-gather.2.cloned.1.call-start = ((), (), s32[]{:S(2)}) async-start(), calls=%async_computation | async-start | bytes 10485760 | tf_op jit(solution)/shard_map/all_gather | solution.py:48
  69.9 8.4 %copy-start = (bf16[4,64,64,256]{3,2,1,0:T(8,128)(2,1)S(1)}, bf16[4,64,64,256]{3,2,1,0:T(8,128)(2,1)}, u32[]{:S(2)}) copy-start(bf16[4,64,64,256]{3,2,1,0:T(8,128)(2,1)} %all-gather.2.cloned.1.call-done) | copy-start | bytes 25165828
  72.8 93.7 %collective-permute-start = (bf16[1,64,64,256]{3,2,1,0:T(8,128)(2,1)S(1)}, bf16[1,64,64,256]{3,2,1,0:T(8,128)(2,1)S(1)}, u32[]{:S(2)}, u32[]{:S(2)}) collective-permute-start(bf16[1,64,64,256]{3,2,1,0:T(8,128)(2,1)S(1)} %get-tuple-element.31), channel_id=1, source_target_pairs={{0,4},{4,8},{8,12},{12,16},{16,20},{20,24},{24,28},{1,5},{5,9},{9,... | collective-permute-start | bytes 6291464 | tf_op jit(solution)/shard_map/ppermute | solution.py:15
  76.5 90.1 %collective-permute-start.1 = (bf16[1,64,64,256]{3,2,1,0:T(8,128)(2,1)S(1)}, bf16[1,64,64,256]{3,2,1,0:T(8,128)(2,1)S(1)}, u32[]{:S(2)}, u32[]{:S(2)}) collective-permute-start(bf16[1,64,64,256]{3,2,1,0:T(8,128)(2,1)S(1)} %get-tuple-element.32), channel_id=1, source_target_pairs={{4,0},{8,4},{12,8},{16,12},{20,16},{24,20},{28,24},{5,1},{9,5},{13... | collective-permute-start | bytes 6291464 | tf_op jit(solution)/shard_map/ppermute | solution.py:17
  349.2 12.8 %slice-start.34 = ((s8[8388608]{0:T(1024)(128)(4,1)}), s8[4194304]{0:T(1024)(128)(4,1)S(1)}, s32[]{:S(2)}) async-start(s8[8388608]{0:T(1024)(128)(4,1)} %bitcast.214), calls=%async_computation.35 | async-start | bytes 8388608
  357.4 9.4 %slice-start.32 = ((s8[8388608]{0:T(1024)(128)(4,1)}), s8[4194304]{0:T(1024)(128)(4,1)S(1)}, s32[]{:S(2)}) async-start(s8[8388608]{0:T(1024)(128)(4,1)} %bitcast.211), calls=%async_computation.33 | async-start | bytes 8388608
  362.1 9.4 %slice-start.30 = ((s8[8388608]{0:T(1024)(128)(4,1)}), s8[4194304]{0:T(1024)(128)(4,1)S(1)}, s32[]{:S(2)}) async-start(s8[8388608]{0:T(1024)(128)(4,1)} %bitcast.208), calls=%async_computation.31 | async-start | bytes 8388608
  366.8 9.3 %slice-start.28 = ((s8[8388608]{0:T(1024)(128)(4,1)}), s8[4194304]{0:T(1024)(128)(4,1)S(1)}, s32[]{:S(2)}) async-start(s8[8388608]{0:T(1024)(128)(4,1)} %bitcast.205), calls=%async_computation.29 | async-start | bytes 8388608
  371.5 9.3 %slice-start.26 = ((s8[8388608]{0:T(1024)(128)(4,1)}), s8[4194304]{0:T(1024)(128)(4,1)S(1)}, s32[]{:S(2)}) async-start(s8[8388608]{0:T(1024)(128)(4,1)} %bitcast.202), calls=%async_computation.27 | async-start | bytes 8388608
  376.1 9.3 %slice-start.24 = ((s8[8388608]{0:T(1024)(128)(4,1)}), s8[4194304]{0:T(1024)(128)(4,1)S(1)}, s32[]{:S(2)}) async-start(s8[8388608]{0:T(1024)(128)(4,1)} %bitcast.199), calls=%async_computation.25 | async-start | bytes 8388608
  380.7 9.3 %slice-start.42 = ((s8[8388608]{0:T(1024)(128)(4,1)}), s8[4194304]{0:T(1024)(128)(4,1)S(1)}, s32[]{:S(2)}) async-start(s8[8388608]{0:T(1024)(128)(4,1)} %bitcast.228), calls=%async_computation.43 | async-start | bytes 8388608
  385.4 9.4 %slice-start.40 = ((s8[8388608]{0:T(1024)(128)(4,1)}), s8[4194304]{0:T(1024)(128)(4,1)S(1)}, s32[]{:S(2)}) async-start(s8[8388608]{0:T(1024)(128)(4,1)} %bitcast.225), calls=%async_computation.41 | async-start | bytes 8388608
  390.0 9.4 %slice-start.38 = ((s8[8388608]{0:T(1024)(128)(4,1)}), s8[4194304]{0:T(1024)(128)(4,1)S(1)}, s32[]{:S(2)}) async-start(s8[8388608]{0:T(1024)(128)(4,1)} %bitcast.222), calls=%async_computation.39 | async-start | bytes 8388608
  394.8 9.4 %slice-start = ((s8[8388608]{0:T(1024)(128)(4,1)}), s8[4194304]{0:T(1024)(128)(4,1)S(1)}, s32[]{:S(2)}) async-start(s8[8388608]{0:T(1024)(128)(4,1)} %bitcast.164), calls=%async_computation.1 | async-start | bytes 8388608
  399.4 13.8 %slice-start.22 = ((s8[8388608]{0:T(1024)(128)(4,1)}), s8[4194304]{0:T(1024)(128)(4,1)S(1)}, s32[]{:S(2)}) async-start(s8[8388608]{0:T(1024)(128)(4,1)} %bitcast.196), calls=%async_computation.23 | async-start | bytes 8388608
  404.2 9.0 %slice-start.23 = ((s8[8388608]{0:T(1024)(128)(4,1)}), s8[4194304]{0:T(1024)(128)(4,1)S(1)}, s32[]{:S(2)}) async-start(s8[8388608]{0:T(1024)(128)(4,1)} %bitcast.196), calls=%async_computation.24 | async-start | bytes 8388608
  408.6 9.2 %slice-start.20 = ((s8[8388608]{0:T(1024)(128)(4,1)}), s8[4194304]{0:T(1024)(128)(4,1)S(1)}, s32[]{:S(2)}) async-start(s8[8388608]{0:T(1024)(128)(4,1)} %bitcast.193), calls=%async_computation.21 | async-start | bytes 8388608
  413.2 9.2 %slice-start.18 = ((s8[8388608]{0:T(1024)(128)(4,1)}), s8[4194304]{0:T(1024)(128)(4,1)S(1)}, s32[]{:S(2)}) async-start(s8[8388608]{0:T(1024)(128)(4,1)} %bitcast.190), calls=%async_computation.19 | async-start | bytes 8388608
  417.8 9.2 %slice-start.16 = ((s8[8388608]{0:T(1024)(128)(4,1)}), s8[4194304]{0:T(1024)(128)(4,1)S(1)}, s32[]{:S(2)}) async-start(s8[8388608]{0:T(1024)(128)(4,1)} %bitcast.187), calls=%async_computation.17 | async-start | bytes 8388608
  422.4 9.2 %slice-start.14 = ((s8[8388608]{0:T(1024)(128)(4,1)}), s8[4194304]{0:T(1024)(128)(4,1)S(1)}, s32[]{:S(2)}) async-start(s8[8388608]{0:T(1024)(128)(4,1)} %bitcast.184), calls=%async_computation.15 | async-start | bytes 8388608
  427.0 9.2 %slice-start.10 = ((s8[8388608]{0:T(1024)(128)(4,1)}), s8[4194304]{0:T(1024)(128)(4,1)S(1)}, s32[]{:S(2)}) async-start(s8[8388608]{0:T(1024)(128)(4,1)} %bitcast.178), calls=%async_computation.11 | async-start | bytes 8388608
  431.6 9.2 %slice-start.8 = ((s8[8388608]{0:T(1024)(128)(4,1)}), s8[4194304]{0:T(1024)(128)(4,1)S(1)}, s32[]{:S(2)}) async-start(s8[8388608]{0:T(1024)(128)(4,1)} %bitcast.175), calls=%async_computation.9 | async-start | bytes 8388608
  436.2 9.2 %slice-start.6 = ((s8[8388608]{0:T(1024)(128)(4,1)}), s8[4194304]{0:T(1024)(128)(4,1)S(1)}, s32[]{:S(2)}) async-start(s8[8388608]{0:T(1024)(128)(4,1)} %bitcast.172), calls=%async_computation.7 | async-start | bytes 8388608
  440.8 9.3 %slice-start.4 = ((s8[8388608]{0:T(1024)(128)(4,1)}), s8[4194304]{0:T(1024)(128)(4,1)S(1)}, s32[]{:S(2)}) async-start(s8[8388608]{0:T(1024)(128)(4,1)} %bitcast.169), calls=%async_computation.5 | async-start | bytes 8388608
  445.4 9.4 %slice-start.2 = ((s8[8388608]{0:T(1024)(128)(4,1)}), s8[4194304]{0:T(1024)(128)(4,1)S(1)}, s32[]{:S(2)}) async-start(s8[8388608]{0:T(1024)(128)(4,1)} %bitcast.166), calls=%async_computation.3 | async-start | bytes 8388608
  450.2 9.2 %slice-start.12 = ((s8[8388608]{0:T(1024)(128)(4,1)}), s8[4194304]{0:T(1024)(128)(4,1)S(1)}, s32[]{:S(2)}) async-start(s8[8388608]{0:T(1024)(128)(4,1)} %bitcast.181), calls=%async_computation.13 | async-start | bytes 8388608
  454.8 9.2 %slice-start.36 = ((s8[8388608]{0:T(1024)(128)(4,1)}), s8[4194304]{0:T(1024)(128)(4,1)S(1)}, s32[]{:S(2)}) async-start(s8[8388608]{0:T(1024)(128)(4,1)} %bitcast.217), calls=%async_computation.37 | async-start | bytes 8388608
  464.0 28.8 %slice-start.44 = ((s8[8388608]{0:T(1024)(128)(4,1)}), s8[4194304]{0:T(1024)(128)(4,1)S(1)}, s32[]{:S(2)}) async-start(s8[8388608]{0:T(1024)(128)(4,1)} %bitcast.232), calls=%async_computation.45 | async-start | bytes 8388608
  468.6 24.2 %slice-start.45 = ((s8[8388608]{0:T(1024)(128)(4,1)}), s8[4194304]{0:T(1024)(128)(4,1)S(1)}, s32[]{:S(2)}) async-start(s8[8388608]{0:T(1024)(128)(4,1)} %bitcast.232), calls=%async_computation.46 | async-start | bytes 8388608
  468.6 24.2 %copy-start.7 = (f32[64]{0:T(128)S(1)}, f32[64]{0:T(128)}, u32[]{:S(2)}) copy-start(f32[64]{0:T(128)} %convert_element_type.8) | copy-start | bytes 772
  (26 other events, 118.1 us)
Sparse Core Ops, SparseCore 0:
  8.9 60.9 all-gather.1
where the time goes:
time: 527 us; the launch traced here: 524 us
  local copies, waits for them, and re-layouts  169 us (32%)
  matrix products  163 us (31%)
  waiting for transfers between devices  147 us (28%)
  other arithmetic  26.5 us (5%)
  between operations  14 us (3%)
    dot_general x27, matrix products, convolve(): jnp.einsum('zpi,oi->zpo', window, tap_weight, preferred_element_type=jnp....  163 us
    slice x2, local copies, waits for them, and re-layouts, convolve(): framed[tap_z:tap_z + planes, tap_y:tap_y + rows, tap_x:tap_x + cols]  158 us
    ppermute x1, waiting for transfers between devices, extended(): lax.ppermute(tail, axis, [(i, (i + 1) % count) for i in range(ends)])  83.6 us
    all_gather x1, waiting for transfers between devices, body(): slab_planes = lax.all_gather(volume, 'filt', axis=0, tiled=True)  62.7 us
    concatenate x2, other arithmetic, extended(): jnp.concatenate([lax.ppermute(tail, axis, [(i, (i + 1) % count) for i in...  25.9 us
  transfers between devices with their start and end apart: 3, of which 2 were waited for; matrix products, arithmetic and copies ran while one was open for 1% of the time, Pallas kernels for 0%

commit v1 on v0

--- a/solution.py
+++ b/solution.py
@@ -45,7 +45,23 @@
 
 
 def body(volume, weights, bias):
-    slab_planes = lax.all_gather(volume, "filt", axis=0, tiled=True)
+    ways, here, turn = (lax.axis_size("filt"), lax.axis_index("filt"), volume.shape[0])
+    shape = [n * ways if d == 0 else n for d, n in enumerate(volume.shape)]
+    full = lax.dynamic_update_slice_in_dim(
+        jnp.zeros(shape, volume.dtype), volume, here * turn, axis=0
+    )
+    going_up = going_down = volume
+    for far in range(1, ways // 2 + 1):
+        going_up = lax.ppermute(going_up, "filt", [(d, (d + 1) % ways) for d in range(ways)])
+        full = lax.dynamic_update_slice_in_dim(full, going_up, (here - far) % ways * turn, axis=0)
+        if 2 * far < ways:
+            going_down = lax.ppermute(
+                going_down, "filt", [(d, (d - 1) % ways) for d in range(ways)]
+            )
+            full = lax.dynamic_update_slice_in_dim(
+                full, going_down, (here + far) % ways * turn, axis=0
+            )
+    slab_planes = full
     padded = extended(slab_planes, (("slab", 0),), 1)
     return convolve(padded, weights, bias)
 

time: 527 us -> 543 us (1.030); the launches traced: 524 us -> 535 us
  between operations: 14 us -> 0.95 us
  other arithmetic: 26.5 us -> 34.9 us
  starting transfers between devices: 4.93 us -> 11.1 us
  local copies, waits for them, and re-layouts: 169 us -> 175 us
    all_gather x1 -> x0, waiting for transfers between devices: 62.7 us -> none  [body(): slab_planes = lax.all_gather(volume, 'filt', axis=0, tiled=True)]
    ppermute x0 -> x3, waiting for transfers between devices: none -> 62.2 us  [the longest x2 62.2 us: body(): lax.ppermute(going_up, 'filt', [(d, (d + 1) % ways) for d in range(ways)])]
    concatenate x2, other arithmetic: 25.9 us -> 34.4 us  [extended(): jnp.concatenate([lax.ppermute(tail, axis, [(i, (i + 1) % count) for i in...]
    dynamic_update_slice x0 -> x4, local copies, waits for them, and re-layouts: none -> 5.84 us  [the longest x2 3.71 us: body(): lax.dynamic_update_slice_in_dim(full, going_up, (here - far) % ways * tur...]
  transfers between devices with their start and end apart: 3 -> 5, of which waited for: 2 -> 3; matrix products, arithmetic and copies ran while one was open for 1% -> 1% of each run, Pallas kernels for 0% -> 0%
where the time goes in v1:
time: 543 us; the launch traced here: 535 us
  local copies, waits for them, and re-layouts  175 us (32%)
  matrix products  162 us (30%)
  waiting for transfers between devices  150 us (28%)
  other arithmetic  34.9 us (6%)
  starting transfers between devices  11.1 us (2%)
    slice x2, local copies, waits for them, and re-layouts, convolve(): framed[tap_z:tap_z + planes, tap_y:tap_y + rows, tap_x:tap_x + cols]  162 us
    dot_general x27, matrix products, convolve(): jnp.einsum('zpi,oi->zpo', window, tap_weight, preferred_element_type=jnp....  162 us
    ppermute x1, waiting for transfers between devices, extended(): lax.ppermute(tail, axis, [(i, (i + 1) % count) for i in range(ends)])  88.2 us
    ppermute x2, waiting for transfers between devices, body(): lax.ppermute(going_up, 'filt', [(d, (d + 1) % ways) for d in range(ways)])  62.2 us
    concatenate x2, other arithmetic, extended(): jnp.concatenate([lax.ppermute(tail, axis, [(i, (i + 1) % count) for i in...  34.4 us
  transfers between devices with their start and end apart: 5, of which 3 were waited for; matrix products, arithmetic and copies ran while one was open for 1% of the time, Pallas kernels for 0%

profile of v1, /device:TPU:0, one launch (start us, length us, event | category | flops | bytes accessed | tf_op | source)
XLA Modules:
  0.0 534.8 jit_solution(12732265327044835706)
XLA Ops:
  2.5 43.9 %collective-permute-done = bf16[1,64,64,256]{3,2,1,0:T(8,128)(2,1)} collective-permute-done((bf16[1,64,64,256]{3,2,1,0:T(8,128)(2,1)}, bf16[1,64,64,256]{3,2,1,0:T(8,128)(2,1)}, u32[]{:S(2)}, u32[]{:S(2)}) %collective-permute-start) | collective-permute-done | bytes 2097184 | tf_op jit(solution)/shard_map/ppermute | solution.py:55
  53.9 18.3 %collective-permute-done.2 = bf16[1,64,64,256]{3,2,1,0:T(8,128)(2,1)} collective-permute-done((bf16[1,64,64,256]{3,2,1,0:T(8,128)(2,1)}, bf16[1,64,64,256]{3,2,1,0:T(8,128)(2,1)}, u32[]{:S(2)}, u32[]{:S(2)}) %collective-permute-start.2) | collective-permute-done | bytes 2097184 | tf_op jit(solution)/shard_map/ppermute | solution.py:55
  74.4 5.0 collective-permute-start.3
  81.2 88.2 %collective-permute-done.3 = bf16[1,64,64,256]{3,2,1,0:T(8,128)(2,1)S(1)} collective-permute-done((bf16[1,64,64,256]{3,2,1,0:T(8,128)(2,1)S(1)}, bf16[1,64,64,256]{3,2,1,0:T(8,128)(2,1)S(1)}, u32[]{:S(2)}, u32[]{:S(2)}) %collective-permute-start.3) | collective-permute-done | bytes 2097184 | tf_op jit(solution)/shard_map/ppermute | solution.py:15
  172.1 21.5 %select_maximum_fusion = bf16[6,66,66,256]{3,2,1,0:T(8,128)(2,1)} fusion(bf16[1,64,64,256]{3,2,1,0:T(8,128)(2,1)S(1)} %collective-permute-done.4, bf16[4,64,64,256]{3,2,1,0:T(8,128)(2,1)S(1)} %constant_dynamic-update-slice_fusion, bf16[1,64,64,256]{3,2,1,0:T(8,128)(2,1)S(1)} %collective-permute-done.3), kind=kLoop, calls=%fused_computation.7 | loop fusion | flops 127125504 | bytes 25964544 | tf_op jit(solution)/shard_map/concatenate | solution.py:13
  193.6 126.6 %fusion.111 = (bf16[4,64,64,256]{3,2,1,0:T(8,128)(2,1)}, bf16[4,64,64,256]{3,2,1,0:T(8,128)(2,1)}, bf16[4,64,64,256]{3,2,1,0:T(8,128)(2,1)}, bf16[4,64,64,256]{3...) fusion(bf16[6,66,66,256]{3,2,1,0:T(8,128)(2,1)} %select_maximum, ...), kind=kLoop, calls=%fused_computation.126 | loop fusion | bytes 318767104 | tf_op jit(solution)/shard_map/slice | solution.py:35
  320.2 35.6 %fusion.112 = (bf16[4,64,64,256]{3,2,1,0:T(8,128)(2,1)}, bf16[4,64,64,256]{3,2,1,0:T(8,128)(2,1)}, bf16[4,64,64,256]{3,2,1,0:T(8,128)(2,1)}, bf16[4,64,64,256]{3,2,1,0:T(8,128)(2,1)}, bf16[4,64,64,256]{3,2,1,0:T(8,128)(2,1)}) fusion(bf16[6,66,66,256]{3,2,1,0:T(8,128)(2,1)} %select_maximum_fusion), kind=kLoop, calls=%fused_computation.127 | loop fusion | bytes 83886080 | tf_op jit(solution)/shard_map/slice | solution.py:35
  355.8 6.2 %fusion.59 = f32[4,4096,64]{1,2,0:T(8,128)S(1)} fusion(bf16[4,4096,256]{2,1,0:T(8,128)(2,1)} %bitcast.233, bf16[64,27,256]{2,0,1:T(8,128)(2,1)} %param.4), kind=kOutput, calls=%fused_computation.70 | convolution fusion | flops 536870912 | bytes 12615680 | tf_op jit(solution)/shard_map/zpi,oi->zpo/dot_general | solution.py:39
  362.0 5.6 %fusion.61 = f32[4,4096,64]{1,2,0:T(8,128)} fusion(bf16[4,4096,256]{2,1,0:T(8,128)(2,1)S(1)} %bitcast.229, bf16[64,27,256]{2,0,1:T(8,128)(2,1)} %param.4), kind=kOutput, calls=%fused_computation.72 | convolution fusion | flops 536870912 | bytes 12615680 | tf_op jit(solution)/shard_map/zpi,oi->zpo/dot_general | solution.py:39
  367.7 5.6 %fusion.63 = f32[4,4096,64]{1,2,0:T(8,128)} fusion(bf16[4,4096,256]{2,1,0:T(8,128)(2,1)S(1)} %bitcast.225, bf16[64,27,256]{2,0,1:T(8,128)(2,1)} %param.4), kind=kOutput, calls=%fused_computation.74 | convolution fusion | flops 536870912 | bytes 12615680 | tf_op jit(solution)/shard_map/zpi,oi->zpo/dot_general | solution.py:39
  373.3 5.5 %fusion.65 = f32[4,4096,64]{1,2,0:T(8,128)} fusion(bf16[4,4096,256]{2,1,0:T(8,128)(2,1)S(1)} %bitcast.219, bf16[64,27,256]{2,0,1:T(8,128)(2,1)} %param.4), kind=kOutput, calls=%fused_computation.76 | convolution fusion | flops 536870912 | bytes 12615680 | tf_op jit(solution)/shard_map/zpi,oi->zpo/dot_general | solution.py:39
  378.7 5.5 %fusion.67 = f32[4,4096,64]{1,2,0:T(8,128)} fusion(bf16[4,4096,256]{2,1,0:T(8,128)(2,1)S(1)} %bitcast.213, bf16[64,27,256]{2,0,1:T(8,128)(2,1)} %param.4), kind=kOutput, calls=%fused_computation.78 | convolution fusion | flops 536870912 | bytes 12615680 | tf_op jit(solution)/shard_map/zpi,oi->zpo/dot_general | solution.py:39
  384.3 5.5 %fusion.69 = f32[4,4096,64]{1,2,0:T(8,128)} fusion(bf16[4,4096,256]{2,1,0:T(8,128)(2,1)S(1)} %bitcast.210, bf16[64,27,256]{2,0,1:T(8,128)(2,1)} %param.4), kind=kOutput, calls=%fused_computation.80 | convolution fusion | flops 536870912 | bytes 12615680 | tf_op jit(solution)/shard_map/zpi,oi->zpo/dot_general | solution.py:39
  389.9 4.8 fusion.71
  394.7 12.9 %pad_maximum_fusion.1 = (bf16[4,64,64,256]{3,2,1,0:T(8,128)(2,1)S(1)}, bf16[4,64,64,256]{3,2,1,0:T(8,128)(2,1)}) fusion(bf16[4,64,64,256]{3,2,1,0:T(8,128)(2,1)S(1)} %bitcast.165, bf16[1,64,64,256]{3,2,1,0:T(8,128)(2,1)S(1)} %copy-done.3, bf16[1,64,64,256]{3,2,1,0:T(8,128)(2,1)S(1)} %copy-done.5), kind=kLoop, calls=%fused_computation.14 | loop fusion | flops 8388608 | bytes 29360128 | tf_op jit(solution)/shard_map/concatenate | solution.py:13
  407.6 4.6 fusion.75
  412.2 4.6 fusion.73
  416.8 4.6 fusion.77
  421.4 4.6 fusion.79
  426.1 4.6 fusion.81
  430.7 4.6 fusion.34
  439.9 4.6 fusion.38
  444.5 4.8 fusion.42
  449.2 4.7 fusion.44
  458.5 4.6 fusion.48
  463.1 4.7 fusion.50
  467.8 4.6 fusion.52
  477.0 4.6 fusion.56
  481.6 4.7 fusion.40
  486.2 4.9 fusion.32
  491.1 18.2 %fusion.23 = f32[4,4096,64]{1,2,0:T(8,128)} fusion(f32[4,4096,64]{1,2,0:T(8,128)S(1)} %fusion.59, f32[4,4096,64]{1,2,0:T(8,128)} %fusion.61, f32[4,4096,64]{1,2,0:T(8,128)} %fusion.63, f32[4,4096,64]{1,2,0:T(8,128)} %fusion.65, f32[4,4096,64]{1,2,0:T(8,128)} %fusion.67, f32[4,4096,64]{1,2,0:T(8,128)} %fusion.69, f32[4,4096,64]{1,2,0:T(8,128)} %fusion.71, ...), kind=kOutput, calls=%fused_computation.34 | convolution fusion | flops 549453824 | bytes 62947328 | tf_op jit(solution)/shard_map/zpi,oi->zpo/dot_general | solution.py:39
  509.3 22.0 %fusion.31 = bf16[4,4096,64]{1,2,0:T(8,128)(2,1)S(1)} fusion(f32[4,4096,64]{1,2,0:T(8,128)} %fusion.32, f32[4,4096,64]{1,2,0:T(8,128)} %fusion.34, f32[4,4096,64]{1,2,0:T(8,128)} %fusion.36, f32[4,4096,64]{1,2,0:T(8,128)} %fusion.38, f32[4,4096,64]{1,2,0:T(8,128)} %fusion.40, f32[4,4096,64]{1,2,0:T(8,128)} %fusion.42, f32[4,4096,64]{1,2,0:T(8,128)} %fusion.44, ...), kind=kOutput, calls=%fused_computation.42 | convolution fusion | flops 556793856 | bytes 69239040 | tf_op jit(solution)/shard_map/zpi,oi->zpo/dot_general | solution.py:39
  (157 shorter events, 33.6 us)
Async XLA Ops:
  0.0 49.8 %copy-start.6 = (bf16[1,64,64,256]{3,2,1,0:T(8,128)(2,1)S(1)}, bf16[1,64,64,256]{3,2,1,0:T(8,128)(2,1)}, u32[]{:S(2)}) copy-start(bf16[1,64,64,256]{3,2,1,0:T(8,128)(2,1)} %param.3) | copy-start | bytes 6291460
  0.0 46.4 %collective-permute-start = (bf16[1,64,64,256]{3,2,1,0:T(8,128)(2,1)}, bf16[1,64,64,256]{3,2,1,0:T(8,128)(2,1)}, u32[]{:S(2)}, u32[]{:S(2)}) collective-permute-start(bf16[1,64,64,256]{3,2,1,0:T(8,128)(2,1)} %param.3), channel_id=1, source_target_pairs={{0,1},{1,2},{2,3},{3,0},{4,5},{5,6},{6,7},{7,4},{8,9},{9,10},{10,1... | collective-permute-start | bytes 6291464 | tf_op jit(solution)/shard_map/ppermute | solution.py:55
  0.5 51.6 %collective-permute-start.1 = (bf16[1,64,64,256]{3,2,1,0:T(8,128)(2,1)}, bf16[1,64,64,256]{3,2,1,0:T(8,128)(2,1)}, u32[]{:S(2)}, u32[]{:S(2)}) collective-permute-start(bf16[1,64,64,256]{3,2,1,0:T(8,128)(2,1)} %param.3), channel_id=1, source_target_pairs={{0,3},{1,0},{2,1},{3,2},{4,7},{5,4},{6,5},{7,6},{8,11},{9,8},{10,9... | collective-permute-start | bytes 6291464 | tf_op jit(solution)/shard_map/ppermute | solution.py:58
  46.4 25.8 %collective-permute-start.2 = (bf16[1,64,64,256]{3,2,1,0:T(8,128)(2,1)}, bf16[1,64,64,256]{3,2,1,0:T(8,128)(2,1)}, u32[]{:S(2)}, u32[]{:S(2)}) collective-permute-start(bf16[1,64,64,256]{3,2,1,0:T(8,128)(2,1)} %collective-permute-done), channel_id=1, source_target_pairs={{0,1},{1,2},{2,3},{3,0},{4,5},{5,6},{6,7},{7,4},{8,9},{9,10},{10,1... | collective-permute-start | bytes 6291464 | tf_op jit(solution)/shard_map/ppermute | solution.py:55
  52.0 28.6 %copy-start.9 = (bf16[64]{0:T(256)(128)(2,1)S(1)}, bf16[64]{0:T(256)(128)(2,1)}, u32[]{:S(2)}) copy-start(bf16[64]{0:T(256)(128)(2,1)} %param.5) | copy-start | bytes 388
  74.0 95.4 %copy-start = (bf16[4,64,64,256]{3,2,1,0:T(8,128)(2,1)}, bf16[4,64,64,256]{3,2,1,0:T(8,128)(2,1)S(1)}, u32[]{:S(2)}) copy-start(bf16[4,64,64,256]{3,2,1,0:T(8,128)(2,1)S(1)} %constant_dynamic-update-slice_fusion) | copy-start | bytes 25165828
  74.4 95.1 %collective-permute-start.3 = (bf16[1,64,64,256]{3,2,1,0:T(8,128)(2,1)S(1)}, bf16[1,64,64,256]{3,2,1,0:T(8,128)(2,1)S(1)}, u32[]{:S(2)}, u32[]{:S(2)}) collective-permute-start(bf16[1,64,64,256]{3,2,1,0:T(8,128)(2,1)S(1)} %get-tuple-element.31), channel_id=1, source_target_pairs={{0,4},{4,8},{8,12},{12,16},{16,20},{20,24},{24,28},{1,5},{5,9},{9,... | collective-permute-start | bytes 6291464 | tf_op jit(solution)/shard_map/ppermute | solution.py:15
  79.3 90.1 %collective-permute-start.4 = (bf16[1,64,64,256]{3,2,1,0:T(8,128)(2,1)S(1)}, bf16[1,64,64,256]{3,2,1,0:T(8,128)(2,1)S(1)}, u32[]{:S(2)}, u32[]{:S(2)}) collective-permute-start(bf16[1,64,64,256]{3,2,1,0:T(8,128)(2,1)S(1)} %get-tuple-element.32), channel_id=1, source_target_pairs={{4,0},{8,4},{12,8},{16,12},{20,16},{24,20},{28,24},{5,1},{9,5},{13... | collective-permute-start | bytes 6291464 | tf_op jit(solution)/shard_map/ppermute | solution.py:17
  355.8 11.8 %slice-start.40 = ((s8[8388608]{0:T(1024)(128)(4,1)}), s8[4194304]{0:T(1024)(128)(4,1)S(1)}, s32[]{:S(2)}) async-start(s8[8388608]{0:T(1024)(128)(4,1)} %bitcast.223), calls=%async_computation.40 | async-start | bytes 8388608
  362.0 11.3 %slice-start.36 = ((s8[8388608]{0:T(1024)(128)(4,1)}), s8[4194304]{0:T(1024)(128)(4,1)S(1)}, s32[]{:S(2)}) async-start(s8[8388608]{0:T(1024)(128)(4,1)} %bitcast.217), calls=%async_computation.36 | async-start | bytes 8388608
  367.6 11.1 %slice-start.32 = ((s8[8388608]{0:T(1024)(128)(4,1)}), s8[4194304]{0:T(1024)(128)(4,1)S(1)}, s32[]{:S(2)}) async-start(s8[8388608]{0:T(1024)(128)(4,1)} %bitcast.211), calls=%async_computation.32 | async-start | bytes 8388608
  373.2 11.0 %slice-start.30 = ((s8[8388608]{0:T(1024)(128)(4,1)}), s8[4194304]{0:T(1024)(128)(4,1)S(1)}, s32[]{:S(2)}) async-start(s8[8388608]{0:T(1024)(128)(4,1)} %bitcast.208), calls=%async_computation.30 | async-start | bytes 8388608
  378.7 11.1 %slice-start.28 = ((s8[8388608]{0:T(1024)(128)(4,1)}), s8[4194304]{0:T(1024)(128)(4,1)S(1)}, s32[]{:S(2)}) async-start(s8[8388608]{0:T(1024)(128)(4,1)} %bitcast.205), calls=%async_computation.28 | async-start | bytes 8388608
  384.3 10.4 %slice-start = ((s8[8388608]{0:T(1024)(128)(4,1)}), s8[4194304]{0:T(1024)(128)(4,1)S(1)}, s32[]{:S(2)}) async-start(s8[8388608]{0:T(1024)(128)(4,1)} %bitcast.164), calls=%async_computation | async-start | bytes 8388608
  389.9 22.3 %slice-start.44 = ((s8[8388608]{0:T(1024)(128)(4,1)}), s8[4194304]{0:T(1024)(128)(4,1)S(1)}, s32[]{:S(2)}) async-start(s8[8388608]{0:T(1024)(128)(4,1)} %bitcast.230), calls=%async_computation.44 | async-start | bytes 8388608
  394.7 17.5 %slice-start.45 = ((s8[8388608]{0:T(1024)(128)(4,1)}), s8[4194304]{0:T(1024)(128)(4,1)S(1)}, s32[]{:S(2)}) async-start(s8[8388608]{0:T(1024)(128)(4,1)} %bitcast.230), calls=%async_computation.45 | async-start | bytes 8388608
  407.6 9.2 %slice-start.42 = ((s8[8388608]{0:T(1024)(128)(4,1)}), s8[4194304]{0:T(1024)(128)(4,1)S(1)}, s32[]{:S(2)}) async-start(s8[8388608]{0:T(1024)(128)(4,1)} %bitcast.226), calls=%async_computation.42 | async-start | bytes 8388608
  412.2 9.2 %slice-start.38 = ((s8[8388608]{0:T(1024)(128)(4,1)}), s8[4194304]{0:T(1024)(128)(4,1)S(1)}, s32[]{:S(2)}) async-start(s8[8388608]{0:T(1024)(128)(4,1)} %bitcast.220), calls=%async_computation.38 | async-start | bytes 8388608
  416.8 9.2 %slice-start.34 = ((s8[8388608]{0:T(1024)(128)(4,1)}), s8[4194304]{0:T(1024)(128)(4,1)S(1)}, s32[]{:S(2)}) async-start(s8[8388608]{0:T(1024)(128)(4,1)} %bitcast.214), calls=%async_computation.34 | async-start | bytes 8388608
  421.4 9.2 %slice-start.24 = ((s8[8388608]{0:T(1024)(128)(4,1)}), s8[4194304]{0:T(1024)(128)(4,1)S(1)}, s32[]{:S(2)}) async-start(s8[8388608]{0:T(1024)(128)(4,1)} %bitcast.199), calls=%async_computation.24 | async-start | bytes 8388608
  426.1 9.2 %slice-start.22 = ((s8[8388608]{0:T(1024)(128)(4,1)}), s8[4194304]{0:T(1024)(128)(4,1)S(1)}, s32[]{:S(2)}) async-start(s8[8388608]{0:T(1024)(128)(4,1)} %bitcast.196), calls=%async_computation.22 | async-start | bytes 8388608
  430.7 9.2 %slice-start.20 = ((s8[8388608]{0:T(1024)(128)(4,1)}), s8[4194304]{0:T(1024)(128)(4,1)S(1)}, s32[]{:S(2)}) async-start(s8[8388608]{0:T(1024)(128)(4,1)} %bitcast.193), calls=%async_computation.20 | async-start | bytes 8388608
  435.3 9.2 %slice-start.18 = ((s8[8388608]{0:T(1024)(128)(4,1)}), s8[4194304]{0:T(1024)(128)(4,1)S(1)}, s32[]{:S(2)}) async-start(s8[8388608]{0:T(1024)(128)(4,1)} %bitcast.190), calls=%async_computation.18 | async-start | bytes 8388608
  439.9 9.4 %slice-start.16 = ((s8[8388608]{0:T(1024)(128)(4,1)}), s8[4194304]{0:T(1024)(128)(4,1)S(1)}, s32[]{:S(2)}) async-start(s8[8388608]{0:T(1024)(128)(4,1)} %bitcast.187), calls=%async_computation.16 | async-start | bytes 8388608
  444.5 9.5 %slice-start.14 = ((s8[8388608]{0:T(1024)(128)(4,1)}), s8[4194304]{0:T(1024)(128)(4,1)S(1)}, s32[]{:S(2)}) async-start(s8[8388608]{0:T(1024)(128)(4,1)} %bitcast.184), calls=%async_computation.14 | async-start | bytes 8388608
  449.2 9.3 %slice-start.12 = ((s8[8388608]{0:T(1024)(128)(4,1)}), s8[4194304]{0:T(1024)(128)(4,1)S(1)}, s32[]{:S(2)}) async-start(s8[8388608]{0:T(1024)(128)(4,1)} %bitcast.181), calls=%async_computation.12 | async-start | bytes 8388608
  458.5 9.3 %slice-start.6 = ((s8[8388608]{0:T(1024)(128)(4,1)}), s8[4194304]{0:T(1024)(128)(4,1)S(1)}, s32[]{:S(2)}) async-start(s8[8388608]{0:T(1024)(128)(4,1)} %bitcast.172), calls=%async_computation.6 | async-start | bytes 8388608
  463.1 9.3 %slice-start.4 = ((s8[8388608]{0:T(1024)(128)(4,1)}), s8[4194304]{0:T(1024)(128)(4,1)S(1)}, s32[]{:S(2)}) async-start(s8[8388608]{0:T(1024)(128)(4,1)} %bitcast.169), calls=%async_computation.4 | async-start | bytes 8388608
  472.4 9.2 %slice-start.26 = ((s8[8388608]{0:T(1024)(128)(4,1)}), s8[4194304]{0:T(1024)(128)(4,1)S(1)}, s32[]{:S(2)}) async-start(s8[8388608]{0:T(1024)(128)(4,1)} %bitcast.202), calls=%async_computation.26 | async-start | bytes 8388608
  476.9 9.3 %slice-start.8 = ((s8[8388608]{0:T(1024)(128)(4,1)}), s8[4194304]{0:T(1024)(128)(4,1)S(1)}, s32[]{:S(2)}) async-start(s8[8388608]{0:T(1024)(128)(4,1)} %bitcast.175), calls=%async_computation.8 | async-start | bytes 8388608
  481.5 9.6 %slice-start.46 = ((s8[8388608]{0:T(1024)(128)(4,1)}), s8[4194304]{0:T(1024)(128)(4,1)S(1)}, s32[]{:S(2)}) async-start(s8[8388608]{0:T(1024)(128)(4,1)} %bitcast.235), calls=%async_computation.46 | async-start | bytes 8388608
  491.1 18.2 %copy-start.8 = (f32[64]{0:T(128)S(1)}, f32[64]{0:T(128)}, u32[]{:S(2)}) copy-start(f32[64]{0:T(128)} %convert_element_type.8) | copy-start | bytes 772
  (31 other events, 153.9 us)
